TPU v7x, 512 devices: a whole 4x4x16 slice. The times are simulated.
512 devices in a mesh: seq: 64 (over z_lo, x, core), chan: 8 (over z_hi, y).
Axes of the slice: x: 4, y: 4, z: 16 (z_hi: 2, z_lo: 8; z = z_hi * 8 + z_lo), core: 2. Of those that a mesh axis runs over, the one named last changes fastest.
Arguments:
- inputs: bfloat16 [512, 262144], P('chan', 'seq'), may hold values from -6 to 6
- gate_acts: bfloat16 [512, 262144], P('chan', 'seq'), may hold values from -6 to 6
- out_grad: bfloat16 [512, 262144], P('chan', 'seq'), may hold values from -6 to 6
- first_factor: bfloat16 [512, 512], replicated, may hold values from -0.25 to 0.25
- second_factor: bfloat16 [512, 512], replicated, may hold values from -0.25 to 0.25
Outputs:
- input_grad: bfloat16 [512, 262144], P('chan', 'seq')
- gate_grad: bfloat16 [512, 262144], P('chan', 'seq')
- first_grad: float32 [512, 512], P('seq')
- second_grad: float32 [512, 512], P('seq')
All inputs are finite; a program needn't handle non-finite values.
Results may differ from a plain program's by a relative error of at most 0.0057.
Values may be sent and summed in bfloat16 or wider, within the bound.
No kernel may reach another device: no remote copies, remote signals or barrier semaphores. Data moves between devices by JAX's collectives and lax.ppermute only.
A program may use at most 64 MiB of HBM per device.

v0:
```python
import jax
import jax.numpy as jnp
from jax import lax
from jax.sharding import PartitionSpec as P


def reduce_factors(first_term, second_term):
    totals = lax.psum((first_term, second_term), "chan")
    return (
        lax.psum_scatter(totals[0], "seq", scatter_dimension=0, tiled=True),
        lax.psum_scatter(totals[1], "seq", scatter_dimension=0, tiled=True),
    )


def local(inputs, gate_acts, out_grad, first_factor, second_factor):
    sequence_count = lax.axis_size("seq")
    chan_width, local_extent = inputs.shape
    cols_total = first_factor.shape[0]
    rows_total = second_factor.shape[0]
    row_block = rows_total // sequence_count
    col_block = cols_total // sequence_count
    grid_rows = inputs.reshape(chan_width, row_block, cols_total)
    first_blocks = first_factor.reshape(sequence_count, col_block, cols_total)
    second_block_list = second_factor.reshape(rows_total, sequence_count, row_block)
    outgoing_grid = jnp.einsum(
        "cij,skj->skic", grid_rows, first_blocks, preferred_element_type=jnp.float32
    ).astype(jnp.bfloat16)
    received_grid = lax.all_to_all(
        outgoing_grid.reshape(sequence_count, -1), "seq", split_axis=0, concat_axis=0, tiled=True
    )
    received_grid = received_grid.reshape(sequence_count, col_block, row_block, chan_width)
    mixed_out = jnp.einsum(
        "odgi,fog->idf", received_grid, second_block_list, preferred_element_type=jnp.float32
    )
    gate_vals = gate_acts.reshape(chan_width, col_block, rows_total).astype(jnp.float32)
    gradient_entries = out_grad.reshape(chan_width, col_block, rows_total).astype(jnp.float32)
    gate_grad = (
        (gradient_entries * mixed_out).astype(jnp.bfloat16).reshape(chan_width, local_extent)
    )
    mixer_gradient = (gradient_entries * gate_vals).astype(jnp.bfloat16)
    back_grid = jnp.einsum(
        "vph,hox->opxv", mixer_gradient, second_block_list, preferred_element_type=jnp.float32
    ).astype(jnp.bfloat16)
    second_term = jnp.einsum(
        "wjq,ajtw->qat", mixer_gradient, received_grid, preferred_element_type=jnp.float32
    ).reshape(rows_total, rows_total)
    returned = lax.all_to_all(
        back_grid.reshape(sequence_count, -1), "seq", split_axis=0, concat_axis=0, tiled=True
    )
    returned = returned.reshape(sequence_count, col_block, row_block, chan_width)
    input_grad = jnp.einsum(
        "skrc,skj->crj", returned, first_blocks, preferred_element_type=jnp.float32
    )
    input_grad = input_grad.astype(jnp.bfloat16).reshape(chan_width, local_extent)
    first_term = jnp.einsum(
        "skrc,crj->skj", returned, grid_rows, preferred_element_type=jnp.float32
    ).reshape(cols_total, cols_total)
    first_grad, second_grad = reduce_factors(first_term, second_term)
    return (input_grad, gate_grad, first_grad, second_grad)


def solution(mesh):
    return jax.shard_map(
        local,
        mesh=mesh,
        in_specs=(P("chan", "seq"), P("chan", "seq"), P("chan", "seq"), P(), P()),
        out_specs=(P("chan", "seq"), P("chan", "seq"), P("seq", None), P("seq", None)),
        check_vma=False,
    )
```

profile of v0, /device:TPU:1, one launch (start us, length us, event | category | flops | bytes accessed | tf_op | source)
XLA Modules:
  0.0 1026.2 jit_solution(3823904096817108904)
XLA Ops:
  7.2 1.4 copy.31
  8.6 0.0 copy-done.3
  8.6 0.1 multiply_convert_fusion
  8.7 0.2 copy.55
  8.9 0.5 copy-done.6
  9.4 0.8 fusion
  10.2 2.1 copy.33
  12.3 0.7 all_to_all.16
  12.9 0.5 broadcast.1
  13.5 3.8 reduce.1
  17.3 1.2 reshape.70
  18.4 17.2 %all-to-all-start = ((bf16[64,2,2048]{2,1,0:T(2,128)(2,1)}), bf16[64,2,2048]{2,1,0:T(2,128)(2,1)}, u32[]{:S(2)}, u32[]{:S(2)}) async-start(bf16[64,2,2048]{2,1,0:T(2,128)(2,1)} %reshape.70), calls=%async_computation | async-start | bytes 1048576 | tf_op jit(solution)/shard_map/all_to_all | solution.py:47
  35.7 1.0 copy.56
  36.7 0.7 fusion.1
  37.4 0.3 copy.38
  37.7 0.7 all_to_all.17
  38.4 3.8 reduce.2
  42.2 1.2 reshape.72
  43.3 22.4 %all-to-all-done = bf16[64,2,2048]{2,1,0:T(2,128)(2,1)} async-done(((bf16[64,2,2048]{2,1,0:T(2,128)(2,1)}), bf16[64,2,2048]{2,1,0:T(2,128)(2,1)}, u32[]{:S(2)}, u32[]{:S(2)}) %all-to-all-start) | async-done | bytes 524320 | tf_op jit(solution)/shard_map/all_to_all | solution.py:47
  65.7 6.8 all-to-all-start.1
  72.6 0.3 reduce-scatter.3.cloned.1.call-start
  72.8 3.6 reshape.71
  76.5 3.1 reduce
  79.6 1.1 reshape.51
  80.8 1.3 copy.44
  82.1 1.5 convolution_bitcast_fusion.1
  83.5 0.0 reduce-scatter.3.cloned.1.call-update
  83.5 0.0 reduce-scatter.5.cloned.1.call-start
  83.6 0.1 convert_element_type.47
  83.7 0.6 copy.57
  84.3 0.4 copy-done.4
  84.7 0.2 copy.58
  84.9 0.1 fusion.7
  85.0 17.6 %all-to-all-done.1 = bf16[64,2,2048]{2,1,0:T(2,128)(2,1)} async-done(((bf16[64,2,2048]{2,1,0:T(2,128)(2,1)}), bf16[64,2,2048]{2,1,0:T(2,128)(2,1)}, u32[]{:S(2)}, u32[]{:S(2)}) %all-to-all-start.1) | async-done | bytes 524320 | tf_op jit(solution)/shard_map/all_to_all | solution.py:28
  102.6 4.5 reshape.73
  107.1 3.7 copy.40
  110.8 3.3 copy.45
  114.1 3.1 copy.46
  117.2 2.5 convolution_bitcast_fusion
  119.7 0.0 reduce-scatter.5.cloned.1.call-update
  119.8 0.5 fusion.5
  120.3 0.8 copy.53
  121.2 0.6 copy-done.1
  121.8 0.5 fusion.6
  122.3 0.8 copy.54
  123.2 390.1 %reduce-scatter.3.cloned.1.call-done = f32[8,512]{1,0:T(8,128)} async-done(((f32[512,512]{1,0:T(8,128)}), f32[8,512]{1,0:T(8,128)}) %reduce-scatter.3.cloned.1.call-update) | async-done | bytes 16400 | tf_op jit(solution)/shard_map/reduce_scatter | solution.py:10
  513.3 435.4 %reduce-scatter.5.cloned.1.call-done = f32[8,512]{1,0:T(8,128)} async-done(((f32[512,512]{1,0:T(8,128)}), f32[8,512]{1,0:T(8,128)}) %reduce-scatter.5.cloned.1.call-update) | async-done | bytes 16400 | tf_op jit(solution)/shard_map/reduce_scatter | solution.py:11
  948.7 70.6 %all-reduce = (f32[8,512]{1,0:T(8,128)}, f32[8,512]{1,0:T(8,128)}) all-reduce(f32[8,512]{1,0:T(8,128)} %reduce-scatter.3.cloned.1.call-done, f32[8,512]{1,0:T(8,128)} %reduce-scatter.5.cloned.1.call-done), channel_id=1, replica_groups=mesh['seq'=64,'chan'=8] {'chan'}, use_global_device_ids=true, to_apply=%region_0.0 | all-reduce | flops 8192 | bytes 65536 | tf_op jit(solution)/shard_map/psum | solution.py:8
  (14 shorter events, 0.0 us)
Async XLA Ops:
  7.2 29.5 %copy-start = (bf16[512,512]{1,0:T(8,128)(2,1)S(1)}, bf16[512,512]{1,0:T(8,128)(2,1)}, u32[]{:S(2)}) copy-start(bf16[512,512]{1,0:T(8,128)(2,1)} %param.8) | copy-start | bytes 1572868
  7.2 1.4 copy-start.2
  7.2 1.4 copy-start.3
  8.6 0.8 copy-start.6
  17.3 18.4 %copy-start.5 = (bf16[64,4096]{1,0:T(8,128)(2,1)S(1)}, bf16[64,4096]{1,0:T(8,128)(2,1)}, u32[]{:S(2)}) copy-start(bf16[64,4096]{1,0:T(8,128)(2,1)} %param.5) | copy-start | bytes 1572868
  18.4 47.3 %all-to-all-start = ((bf16[64,2,2048]{2,1,0:T(2,128)(2,1)}), bf16[64,2,2048]{2,1,0:T(2,128)(2,1)}, u32[]{:S(2)}, u32[]{:S(2)}) async-start(bf16[64,2,2048]{2,1,0:T(2,128)(2,1)} %reshape.70), calls=%async_computation | async-start | bytes 1048576 | tf_op jit(solution)/shard_map/all_to_all | solution.py:47
  65.7 36.9 %all-to-all-start.1 = ((bf16[64,2,2048]{2,1,0:T(2,128)(2,1)}), bf16[64,2,2048]{2,1,0:T(2,128)(2,1)}, u32[]{:S(2)}, u32[]{:S(2)}) async-start(bf16[64,2,2048]{2,1,0:T(2,128)(2,1)} %reshape.72), calls=%async_computation.1 | async-start | bytes 1048576 | tf_op jit(solution)/shard_map/all_to_all | solution.py:28
  72.6 440.7 %reduce-scatter.3.cloned.1.call-start = ((), (), s32[]{:S(2)}) async-start(), calls=%async_computation.4 | async-start | bytes 1064960 | tf_op jit(solution)/shard_map/reduce_scatter | solution.py:10
  80.8 1.3 copy-start.8
  83.5 865.2 %reduce-scatter.5.cloned.1.call-start = ((), (), s32[]{:S(2)}) async-start(), calls=%async_computation.5 | async-start | bytes 1064960 | tf_op jit(solution)/shard_map/reduce_scatter | solution.py:11
  83.7 1.0 copy-start.4
  119.8 1.4 copy-start.7
  120.3 1.5 copy-start.1
Sparse Core Ops, SparseCore 0:
  83.7 429.5 reduce-scatter.2
  516.1 432.5 reduce-scatter.4
where the time goes:
time: 1030 us
  waiting for transfers between devices  866 us (84%)
  blocking collectives  70.6 us (7%)
  local copies, waits for them, and re-layouts  33.7 us (3%)
  starting transfers between devices  24.4 us (2%)
  between operations  14.3 us (1%)
  other arithmetic  11 us (1%)
    reduce_scatter x1, waiting for transfers between devices, reduce_factors(): lax.psum_scatter(totals[1], 'seq', scatter_dimension=0, tiled=True)  435 us
    reduce_scatter x1, waiting for transfers between devices, reduce_factors(): lax.psum_scatter(totals[0], 'seq', scatter_dimension=0, tiled=True)  390 us
    psum x1, blocking collectives, reduce_factors(): totals = lax.psum((first_term, second_term), 'chan')  70.6 us
    all_to_all x1, waiting for transfers between devices, local(): lax.all_to_all(back_grid.reshape(sequence_count, -1), 'seq', split_axis=0...  22.4 us
  transfers between devices with their start and end apart: 4, of which 4 were waited for; matrix products, arithmetic and copies ran while one was open for 4% of the time, Pallas kernels for 0%

commit v1 on v0

v1 whole, which is shorter than its diff:
```python
import jax
import jax.numpy as jnp
from jax import lax
from jax.experimental import pallas as pl
from jax.experimental.pallas import tpu as pltpu
from jax.sharding import Mesh
from jax.sharding import PartitionSpec as P

BF = jnp.bfloat16
F32 = jnp.float32
SEQ = ("zl", "x", "core")
CHAN = ("zh", "y")
LANES = 128


def dot(a, b, dims):
    return lax.dot_general(a, b, (dims, ((), ())), preferred_element_type=F32)


def stacked(ref, width):
    blocks = ref.shape[1] // width
    return jnp.concatenate([ref[:, b * width:(b + 1) * width] for b in range(blocks)], axis=0)


def product_stacked(g_ref, q_ref, width):
    blocks = g_ref.shape[1] // width
    return jnp.concatenate(
        [
            (
                g_ref[:, b * width:(b + 1) * width].astype(F32)
                * q_ref[:, b * width:(b + 1) * width].astype(F32)
            ).astype(BF)
            for b in range(blocks)
        ],
        axis=0,
    )


def send_kernel(x_ref, g_ref, q_ref, first_ref, second_ref, out_ref):
    cols = first_ref.shape[0]
    rows = second_ref.shape[0]
    count, both, width = out_ref.shape
    inner = dot(first_ref[...], stacked(x_ref, cols), ((1,), (1,)))
    mixer = product_stacked(g_ref, q_ref, rows)
    back = dot(second_ref[...], mixer, ((0,), (1,)))
    out_ref[...] = jnp.concatenate(
        [inner.reshape(count, both // 2, width), back.reshape(count, both // 2, width)], axis=1
    ).astype(BF)


def regroup(received, scratch, result):
    count, own, width = received.shape
    groups = width // LANES
    half = LANES // 2
    for group in range(groups):
        scratch[group] = received[:, :, group * LANES:(group + 1) * LANES].reshape(count * own, LANES)
    low = lax.broadcasted_iota(jnp.int32, (count, LANES), 1) < half
    for pair in range(own // 2):
        for group in range(groups):
            a = scratch[group, pl.ds(2 * pair, count, stride=own), :]
            b = scratch[group, pl.ds(2 * pair + 1, count, stride=own), :]
            result[pair, pl.ds(2 * group, count, stride=own), :] = jnp.where(low, a, pltpu.roll(b, half, 1))
            result[pair, pl.ds(2 * group + 1, count, stride=own), :] = jnp.where(low, pltpu.roll(a, half, 1), b)
    return jnp.concatenate([result[pair].astype(BF) for pair in range(own // 2)], axis=1)


def terms_kernel(recv_ref, x_ref, g_ref, q_ref, terms_ref, za_ref, zb_ref, scratch, result):
    count, both, width = recv_ref.shape
    own = both // 2
    received = recv_ref[...].astype(F32)
    za = regroup(received[:, :own], scratch, result)
    za_ref[...] = za
    zb = regroup(received[:, own:], scratch, result)
    zb_ref[...] = zb
    mixer = product_stacked(g_ref, q_ref, za.shape[0])
    first = dot(zb, stacked(x_ref, zb.shape[0]), ((1,), (0,)))
    second = dot(mixer, za, ((0,), (1,)))
    targets, lines, lanes = terms_ref.shape
    pieces = first.shape[1] // lanes
    planes = targets // pieces
    for target in range(planes):
        for piece in range(pieces):
            terms_ref[target * pieces + piece] = jnp.concatenate(
                [
                    term[(z * planes + target) * 8:(z * planes + target) * 8 + 8, piece * lanes:(piece + 1) * lanes]
                    for term in (first, second)
                    for z in range(lines // 16)
                ],
                axis=0,
            ).astype(BF)


def grads_kernel(za_ref, zb_ref, g_ref, first_ref, second_ref, input_ref, gate_ref):
    chan = g_ref.shape[0]
    rows = second_ref.shape[0]
    cols = first_ref.shape[0]
    mixed = dot(za_ref[...], second_ref[...], ((0,), (1,)))
    for k in range(mixed.shape[0] // chan):
        span = slice(k * rows, (k + 1) * rows)
        gate_ref[:, span] = (g_ref[:, span].astype(F32) * mixed[k * chan:(k + 1) * chan]).astype(BF)
    grad = dot(zb_ref[...], first_ref[...], ((0,), (0,)))
    for i in range(grad.shape[0] // chan):
        input_ref[:, i * cols:(i + 1) * cols] = grad[i * chan:(i + 1) * chan].astype(BF)


def plane_kernel(recv_ref, out_ref):
    total = recv_ref[0].astype(F32)
    for source in range(1, recv_ref.shape[0]):
        total += recv_ref[source].astype(F32)
    lines = out_ref.shape[0] // 2
    for z in range(lines):
        piece = jnp.concatenate([total[z * 8:z * 8 + 8], total[(lines + z) * 8:(lines + z) * 8 + 8]], axis=0)
        for copy in range(2):
            out_ref[2 * z + copy] = piece.astype(out_ref.dtype)


def line_kernel(recv_ref, out_ref):
    total = recv_ref[0].astype(F32)
    for source in range(1, recv_ref.shape[0]):
        total += recv_ref[source].astype(F32)
    for copy in range(out_ref.shape[0]):
        out_ref[copy] = total


def last_kernel(recv_ref, first_ref, second_ref):
    for piece in range(recv_ref.shape[0]):
        span = slice(piece * LANES, (piece + 1) * LANES)
        first_ref[:, span] = recv_ref[piece, 0:8]
        second_ref[:, span] = recv_ref[piece, 8:16]


def call(kernel, out_shape, name, scratch=(), flops=0, data=0):
    return pl.pallas_call(
        kernel,
        out_shape=out_shape,
        scratch_shapes=scratch,
        name=name,
        cost_estimate=pl.CostEstimate(flops=flops, bytes_accessed=data, transcendentals=0),
        compiler_params=pltpu.CompilerParams(vmem_limit_bytes=40 << 20),
    )


def exchange(value, axes):
    return lax.all_to_all(value, axes, split_axis=0, concat_axis=0, tiled=True)


def local(inputs, gate_acts, out_grad, first_factor, second_factor):
    count = lax.axis_size(SEQ)
    chan, extent = inputs.shape
    cols = first_factor.shape[0]
    rows = second_factor.shape[0]
    own = extent // cols
    width = own * chan
    lines, copies = lax.axis_size("zl"), lax.axis_size("zh")
    pieces = lax.axis_size("y")
    planes = count // lines
    shape = jax.ShapeDtypeStruct
    sent = call(
        send_kernel, shape((count, 2 * own, width), BF), "send", flops=2 * 2 * rows * cols * width, data=5 << 20
    )(inputs, out_grad, gate_acts, first_factor, second_factor)
    received = exchange(sent, SEQ)
    groups = width // LANES
    terms, za, zb = call(
        terms_kernel,
        (
            shape((planes * pieces, 2 * lines * 8, LANES), BF),
            shape((rows, width), BF),
            shape((cols, width), BF),
        ),
        "terms",
        scratch=[pltpu.VMEM((groups, rows, LANES), F32), pltpu.VMEM((own // 2, rows, LANES), F32)],
        flops=2 * 2 * rows * cols * width,
        data=5 << 20,
    )(received, inputs, out_grad, gate_acts)
    plane = exchange(terms, ("x", "core", "y"))
    input_grad, gate_grad = call(
        grads_kernel,
        (shape((chan, extent), BF), shape((chan, extent), BF)),
        "grads",
        flops=2 * 2 * rows * cols * width,
        data=4 << 20,
    )(za, zb, out_grad, first_factor, second_factor)
    partial = call(plane_kernel, shape((lines * copies, 16, LANES), F32), "plane_sum", data=1 << 20)(plane)
    line = exchange(partial, ("zl", "zh"))
    summed = call(line_kernel, shape((pieces, 16, LANES), F32), "line_sum", data=1 << 17)(line)
    gathered = exchange(summed, "y")
    first_grad, second_grad = call(
        last_kernel, (shape((8, cols), F32), shape((8, rows), F32)), "last", data=1 << 16
    )(gathered)
    return (input_grad, gate_grad, first_grad, second_grad)


def solution(mesh):
    fine = Mesh(mesh.devices.reshape(8, 4, 2, 2, 4), SEQ + CHAN)
    return jax.shard_map(
        local,
        mesh=fine,
        in_specs=(P(CHAN, SEQ), P(CHAN, SEQ), P(CHAN, SEQ), P(), P()),
        out_specs=(P(CHAN, SEQ), P(CHAN, SEQ), P(SEQ, None), P(SEQ, None)),
        check_vma=False,
    )
```

time: 1030 us -> 133 us (0.13)
  the two profiles are of different devices: /device:TPU:1 before, /device:TPU:32 now
where the time goes in v1:
time: 133 us; the launch traced here: 132 us
  blocking collectives  114 us (86%)
  Pallas kernels  5.39 us (4%)
  local copies, waits for them, and re-layouts  5.21 us (4%)
  waiting for transfers between devices  3.84 us (3%)
  starting transfers between devices  3.26 us (2%)
    all_to_all x3, blocking collectives, exchange(): return lax.all_to_all(value, axes, split_axis=0, concat_axis=0, tiled=True)  114 us
    unnamed x16, local copies, waits for them, and re-layouts  5.21 us
    all_to_all x1, waiting for transfers between devices, exchange(): return lax.all_to_all(value, axes, split_axis=0, concat_axis=0, tiled=True)  3.84 us
    all_to_all x1, starting transfers between devices, exchange(): return lax.all_to_all(value, axes, split_axis=0, concat_axis=0, tiled=True)  3.26 us
  transfers between devices with their start and end apart: 1, of which 1 were waited for; matrix products, arithmetic and copies ran while one was open for 0% of the time, Pallas kernels for 1%

profile of v1, /device:TPU:32, one launch (start us, length us, event | category | flops | bytes accessed | tf_op | source)
XLA Modules:
  0.0 132.2 jit_solution(8783850318552503616)
XLA Ops:
  0.6 0.0 copy-start
  0.6 1.0 copy-done
  1.7 0.0 copy-start.2
  1.7 1.0 copy-done.2
  2.7 0.0 copy-start.3
  2.7 1.0 copy-done.3
  3.8 0.0 copy-start.4
  3.8 1.0 copy-done.4
  4.8 0.0 copy-start.6
  4.8 1.0 copy-done.6
  5.8 0.7 send.1
  6.6 63.9 %all_to_all.20.recv_ref = bf16[64,16,512]{2,1,0:T(8,128)(2,1)S(1)} all-to-all(bf16[64,16,512]{2,1,0:T(8,128)(2,1)S(1)} %send.1), channel_id=1, replica_groups=mesh['zl'=8,'x'=4,'core'=2,'zh'=2,'y'=4] {'zl','x','core'}, dimensions={0} | all-to-all | bytes 2097152 | tf_op jit(solution)/shard_map/all_to_all | solution.py:144
  70.5 1.7 %terms.1 = (bf16[32,128,128]{2,1,0:T(8,128)(2,1)S(1)}, bf16[512,512]{1,0:T(8,128)(2,1)S(1)}, bf16[512,512]{1,0:T(8,128)(2,1)S(1)}) custom-call(bf16[64,16,512]{2,1,0:T(8,128)(2,1)S(1)} %all_to_all.20.recv_ref, bf16[64,4096]{1,0:T(8,128)(2,1)S(1)} %copy-done.2, bf16[64,4096]{1,0:T(8,128)(2,1)S(1)} %copy-done, bf16[64,4096]{1,0:T(8,128)(2,1)S(1)} %copy-done.3), custom_call_target="tpu_custom_call" | custom-call | flops 536870912 | bytes 5242880 | tf_op jit(solution)/shard_map/terms/pallas_call | solution.py:163
  72.2 26.2 %all_to_all.21.recv_ref = bf16[32,128,128]{2,1,0:T(8,128)(2,1)S(1)} all-to-all(bf16[32,128,128]{2,1,0:T(8,128)(2,1)S(1)} %get-tuple-element.15), channel_id=1, replica_groups=mesh['zl'=8,'x'=4,'core'=2,'zh'=2,'y'=4] {'x','core','y'}, dimensions={0} | all-to-all | bytes 2097152 | tf_op jit(solution)/shard_map/all_to_all | solution.py:144
  98.5 0.0 copy-start.1
  98.5 0.0 copy-start.5
  98.5 0.0 copy-start.7
  98.5 0.2 plane_sum.1
  98.6 23.6 %all_to_all.22.recv_ref = f32[16,16,128]{2,1,0:T(8,128)S(1)} all-to-all(f32[16,16,128]{2,1,0:T(8,128)S(1)} %plane_sum.1), channel_id=1, replica_groups=mesh['zl'=8,'x'=4,'core'=2,'zh'=2,'y'=4] {'zl','zh'}, dimensions={0} | all-to-all | bytes 262144 | tf_op jit(solution)/shard_map/all_to_all | solution.py:144
  122.2 0.6 line_sum.1
  122.9 3.3 %all-to-all-start.3 = ((f32[4,16,128]{2,1,0:T(8,128)}), f32[4,16,128]{2,1,0:T(8,128)S(1)}, u32[]{:S(2)}, u32[]{:S(2)}) async-start(f32[4,16,128]{2,1,0:T(8,128)} %line_sum.1), calls=%async_computation.3 | async-start | bytes 65536 | tf_op jit(solution)/shard_map/all_to_all | solution.py:144
  126.1 0.0 copy-done.1
  126.1 0.0 copy-done.5
  126.2 0.0 copy-done.7
  126.2 1.5 %grads.1 = (bf16[64,4096]{1,0:T(8,128)(2,1)}, bf16[64,4096]{1,0:T(8,128)(2,1)}) custom-call(bf16[512,512]{1,0:T(8,128)(2,1)S(1)} %get-tuple-element.11.za_ref, bf16[512,512]{1,0:T(8,128)(2,1)S(1)} %get-tuple-element.12.zb_ref, bf16[64,4096]{1,0:T(8,128)(2,1)S(1)} %copy-done.1, bf16[512,512]{1,0:T(8,128)(2,1)S(1)} %copy-done.5, bf16[512,512]{1,0:T(8,128)(2,1)S(1)} %copy-done.7), custom_call_target="tpu_custom_call" | custom-call | flops 536870912 | bytes 4194304 | tf_op jit(solution)/shard_map/grads/pallas_call | solution.py:176
  127.7 3.8 %all-to-all-done.3.recv_ref = f32[4,16,128]{2,1,0:T(8,128)S(1)} async-done(((f32[4,16,128]{2,1,0:T(8,128)}), f32[4,16,128]{2,1,0:T(8,128)S(1)}, u32[]{:S(2)}, u32[]{:S(2)}) %all-to-all-start.3) | async-done | bytes 32800 | tf_op jit(solution)/shard_map/all_to_all | solution.py:144
  131.5 0.6 last.1
Async XLA Ops:
  0.6 1.0 copy-start
  1.7 1.0 copy-start.2
  2.7 1.0 copy-start.3
  3.8 1.0 copy-start.4
  4.8 1.0 copy-start.6
  98.5 27.7 %copy-start.1 = (bf16[64,4096]{1,0:T(8,128)(2,1)S(1)}, bf16[64,4096]{1,0:T(8,128)(2,1)}, u32[]{:S(2)}) copy-start(bf16[64,4096]{1,0:T(8,128)(2,1)} %g_ref.5) | copy-start | bytes 1572868
  98.5 27.7 %copy-start.5 = (bf16[512,512]{1,0:T(8,128)(2,1)S(1)}, bf16[512,512]{1,0:T(8,128)(2,1)}, u32[]{:S(2)}) copy-start(bf16[512,512]{1,0:T(8,128)(2,1)} %first_ref.3) | copy-start | bytes 1572868
  98.5 27.7 %copy-start.7 = (bf16[512,512]{1,0:T(8,128)(2,1)S(1)}, bf16[512,512]{1,0:T(8,128)(2,1)}, u32[]{:S(2)}) copy-start(bf16[512,512]{1,0:T(8,128)(2,1)} %second_ref.3) | copy-start | bytes 1572868
  122.9 8.7 %all-to-all-start.3 = ((f32[4,16,128]{2,1,0:T(8,128)}), f32[4,16,128]{2,1,0:T(8,128)S(1)}, u32[]{:S(2)}, u32[]{:S(2)}) async-start(f32[4,16,128]{2,1,0:T(8,128)} %line_sum.1), calls=%async_computation.3 | async-start | bytes 65536 | tf_op jit(solution)/shard_map/all_to_all | solution.py:144

commit v2 on v1

--- a/solution.py
+++ b/solution.py
@@ -36,12 +36,26 @@
     )
 
 
-def send_kernel(x_ref, g_ref, q_ref, first_ref, second_ref, out_ref):
+def send_kernel(
+    x_hbm, g_hbm, q_hbm, first_hbm, second_hbm, out_ref, stack_ref, mixer_ref, x_ref, g_ref, q_ref, first_ref, second_ref, sems
+):
+    pairs = ((x_hbm, x_ref), (first_hbm, first_ref), (g_hbm, g_ref), (q_hbm, q_ref), (second_hbm, second_ref))
+    copies = [pltpu.make_async_copy(src, dst, sems.at[n]) for n, (src, dst) in enumerate(pairs)]
+    for copy in copies:
+        copy.start()
     cols = first_ref.shape[0]
     rows = second_ref.shape[0]
     count, both, width = out_ref.shape
-    inner = dot(first_ref[...], stacked(x_ref, cols), ((1,), (1,)))
+    copies[0].wait()
+    stack = stacked(x_ref, cols)
+    stack_ref[...] = stack
+    copies[1].wait()
+    inner = dot(first_ref[...], stack, ((1,), (1,)))
+    copies[2].wait()
+    copies[3].wait()
     mixer = product_stacked(g_ref, q_ref, rows)
+    mixer_ref[...] = mixer
+    copies[4].wait()
     back = dot(second_ref[...], mixer, ((0,), (1,)))
     out_ref[...] = jnp.concatenate(
         [inner.reshape(count, both // 2, width), back.reshape(count, both // 2, width)], axis=1
@@ -64,7 +78,7 @@
     return jnp.concatenate([result[pair].astype(BF) for pair in range(own // 2)], axis=1)
 
 
-def terms_kernel(recv_ref, x_ref, g_ref, q_ref, terms_ref, za_ref, zb_ref, scratch, result):
+def terms_kernel(recv_ref, stack_ref, mixer_ref, keep_ref, send_ref, za_ref, zb_ref, scratch, result, halves):
     count, both, width = recv_ref.shape
     own = both // 2
     received = recv_ref[...].astype(F32)
@@ -72,22 +86,30 @@
     za_ref[...] = za
     zb = regroup(received[:, own:], scratch, result)
     zb_ref[...] = zb
-    mixer = product_stacked(g_ref, q_ref, za.shape[0])
-    first = dot(zb, stacked(x_ref, zb.shape[0]), ((1,), (0,)))
-    second = dot(mixer, za, ((0,), (1,)))
-    targets, lines, lanes = terms_ref.shape
+    first = dot(zb, stack_ref[...], ((1,), (0,)))
+    second = dot(mixer_ref[...], za, ((0,), (1,)))
+    targets, lines, lanes = keep_ref.shape
     pieces = first.shape[1] // lanes
-    planes = targets // pieces
-    for target in range(planes):
-        for piece in range(pieces):
-            terms_ref[target * pieces + piece] = jnp.concatenate(
-                [
-                    term[(z * planes + target) * 8:(z * planes + target) * 8 + 8, piece * lanes:(piece + 1) * lanes]
-                    for term in (first, second)
-                    for z in range(lines // 16)
-                ],
-                axis=0,
-            ).astype(BF)
+    across = targets // pieces
+    for core in range(2):
+        for x in range(across):
+            for piece in range(pieces):
+                starts = [((z * across + x) * 2 + core) * 8 for z in range(lines // 16)]
+                halves[core, x * pieces + piece] = jnp.concatenate(
+                    [
+                        term[start:start + 8, piece * lanes:(piece + 1) * lanes]
+                        for term in (first, second)
+                        for start in starts
+                    ],
+                    axis=0,
+                )
+    core = lax.axis_index("core")
+    keep_ref[...] = halves[core]
+    send_ref[...] = halves[1 - core].astype(BF)
+
+
+def pair_kernel(keep_ref, recv_ref, out_ref):
+    out_ref[...] = (keep_ref[...] + recv_ref[...].astype(F32)).astype(BF)
 
 
 def grads_kernel(za_ref, zb_ref, g_ref, first_ref, second_ref, input_ref, gate_ref):
@@ -129,14 +151,15 @@
         second_ref[:, span] = recv_ref[piece, 8:16]
 
 
-def call(kernel, out_shape, name, scratch=(), flops=0, data=0):
+def call(kernel, out_shape, name, scratch=(), flops=0, data=0, vmem=40 << 20, **specs):
     return pl.pallas_call(
         kernel,
         out_shape=out_shape,
         scratch_shapes=scratch,
         name=name,
         cost_estimate=pl.CostEstimate(flops=flops, bytes_accessed=data, transcendentals=0),
-        compiler_params=pltpu.CompilerParams(vmem_limit_bytes=40 << 20),
+        compiler_params=pltpu.CompilerParams(vmem_limit_bytes=vmem),
+        **specs,
     )
 
 
@@ -155,24 +178,41 @@
     pieces = lax.axis_size("y")
     planes = count // lines
     shape = jax.ShapeDtypeStruct
-    sent = call(
-        send_kernel, shape((count, 2 * own, width), BF), "send", flops=2 * 2 * rows * cols * width, data=5 << 20
-    )(inputs, out_grad, gate_acts, first_factor, second_factor)
+    given = tuple(
+        pltpu.with_memory_space_constraint(value, pltpu.HBM)
+        for value in (inputs, out_grad, gate_acts, first_factor, second_factor)
+    )
+    sent, stack, mixer = call(
+        send_kernel,
+        (shape((count, 2 * own, width), BF), shape((width, cols), BF), shape((width, rows), BF)),
+        "send",
+        scratch=[pltpu.VMEM(value.shape, BF) for value in given] + [pltpu.SemaphoreType.DMA((len(given),))],
+        flops=2 * 2 * rows * cols * width,
+        data=5 << 20,
+        in_specs=[pl.BlockSpec(memory_space=pltpu.HBM)] * len(given),
+    )(*given)
     received = exchange(sent, SEQ)
     groups = width // LANES
-    terms, za, zb = call(
+    keep, send, za, zb = call(
         terms_kernel,
         (
-            shape((planes * pieces, 2 * lines * 8, LANES), BF),
+            shape((planes // 2 * pieces, 2 * lines * 8, LANES), F32),
+            shape((planes // 2 * pieces, 2 * lines * 8, LANES), BF),
             shape((rows, width), BF),
             shape((cols, width), BF),
         ),
         "terms",
-        scratch=[pltpu.VMEM((groups, rows, LANES), F32), pltpu.VMEM((own // 2, rows, LANES), F32)],
+        scratch=[
+            pltpu.VMEM((groups, rows, LANES), F32),
+            pltpu.VMEM((own // 2, rows, LANES), F32),
+            pltpu.VMEM((2, planes // 2 * pieces, 2 * lines * 8, LANES), F32),
+        ],
         flops=2 * 2 * rows * cols * width,
         data=5 << 20,
-    )(received, inputs, out_grad, gate_acts)
-    plane = exchange(terms, ("x", "core", "y"))
+    )(received, stack, mixer)
+    other = lax.ppermute(send, "core", [(0, 1), (1, 0)])
+    paired = call(pair_kernel, shape(send.shape, BF), "pair_sum", data=2 << 20)(keep, other)
+    plane = exchange(paired, ("x", "y"))
     input_grad, gate_grad = call(
         grads_kernel,
         (shape((chan, extent), BF), shape((chan, extent), BF)),
@@ -180,7 +220,7 @@
         flops=2 * 2 * rows * cols * width,
         data=4 << 20,
     )(za, zb, out_grad, first_factor, second_factor)
-    partial = call(plane_kernel, shape((lines * copies, 16, LANES), F32), "plane_sum", data=1 << 20)(plane)
+    partial = call(plane_kernel, shape((lines * copies, 16, LANES), BF), "plane_sum", data=1 << 20)(plane)
     line = exchange(partial, ("zl", "zh"))
     summed = call(line_kernel, shape((pieces, 16, LANES), F32), "line_sum", data=1 << 17)(line)
     gathered = exchange(summed, "y")

time: 133 us -> 125 us (0.940)
  blocking collectives: 114 us -> 106 us
  local copies, waits for them, and re-layouts: 5.21 us -> 0.02 us
  starting transfers between devices: 3.26 us -> 5.39 us
  Pallas kernels: 5.39 us -> 7.3 us
  waiting for transfers between devices: 3.84 us -> 5.5 us
    all_to_all x3, blocking collectives: 114 us -> 106 us  [exchange(): return lax.all_to_all(value, axes, split_axis=0, concat_axis=0, tiled=True)]
    unnamed x16 -> x6, local copies, waits for them, and re-layouts: 5.21 us -> 0.02 us
    ppermute x0 -> x1, starting transfers between devices: none -> 2.13 us  [local(): other = lax.ppermute(send, 'core', [(0, 1), (1, 0)])]
    pallas_call x3 -> x4, Pallas kernels: 2.6 us -> 4.5 us  [the longest x1 2.36 us: local(): call(send_kernel, (shape((count, 2 * own, width), BF), shape((width, cols...]
    ppermute x0 -> x1, waiting for transfers between devices: none -> 1.67 us  [local(): other = lax.ppermute(send, 'core', [(0, 1), (1, 0)])]
  transfers between devices with their start and end apart: 1 -> 2, of which waited for: 1 -> 2; matrix products, arithmetic and copies ran while one was open for 0% -> 0% of each run, Pallas kernels for 1% -> 1%
where the time goes in v2:
time: 125 us
  blocking collectives  106 us (85%)
  Pallas kernels  7.3 us (6%)
  waiting for transfers between devices  5.5 us (4%)
  starting transfers between devices  5.39 us (4%)
    all_to_all x3, blocking collectives, exchange(): return lax.all_to_all(value, axes, split_axis=0, concat_axis=0, tiled=True)  106 us
    all_to_all x1, waiting for transfers between devices, exchange(): return lax.all_to_all(value, axes, split_axis=0, concat_axis=0, tiled=True)  3.83 us
    all_to_all x1, starting transfers between devices, exchange(): return lax.all_to_all(value, axes, split_axis=0, concat_axis=0, tiled=True)  3.26 us
  transfers between devices with their start and end apart: 2, of which 2 were waited for; matrix products, arithmetic and copies ran while one was open for 0% of the time, Pallas kernels for 1%

profile of v2, /device:TPU:32, one launch (start us, length us, event | category | flops | bytes accessed | tf_op | source)
XLA Modules:
  0.0 124.8 jit_solution(8533356846319663551)
XLA Ops:
  0.6 2.4 %send.1 = (bf16[64,16,512]{2,1,0:T(8,128)(2,1)S(1)}, bf16[512,512]{1,0:T(8,128)(2,1)S(1)}, bf16[512,512]{1,0:T(8,128)(2,1)S(1)}) custom-call(bf16[64,4096]{1,0:T(8,128)(2,1)} %x_hbm.1, bf16[64,4096]{1,0:T(8,128)(2,1)} %g_ref.1, bf16[64,4096]{1,0:T(8,128)(2,1)} %q_hbm.1, bf16[512,512]{1,0:T(8,128)(2,1)} %first_ref.1, bf16[512,512]{1,0:T(8,128)(2,1)} %second_ref.1), custom_call_target="tpu_custom_call" | custom-call | flops 536870912 | bytes 5242880 | tf_op jit(solution)/shard_map/send/pallas_call | solution.py:185
  3.0 63.9 %all_to_all.20.recv_ref = bf16[64,16,512]{2,1,0:T(8,128)(2,1)S(1)} all-to-all(bf16[64,16,512]{2,1,0:T(8,128)(2,1)S(1)} %get-tuple-element.15), channel_id=1, replica_groups=mesh['zl'=8,'x'=4,'core'=2,'zh'=2,'y'=4] {'zl','x','core'}, dimensions={0} | all-to-all | bytes 2097152 | tf_op jit(solution)/shard_map/all_to_all | solution.py:167
  66.9 2.0 %terms.1 = (f32[16,128,128]{2,1,0:T(8,128)S(1)}, bf16[16,128,128]{2,1,0:T(8,128)(2,1)S(1)}, bf16[512,512]{1,0:T(8,128)(2,1)S(1)}, bf16[512,512]{1,0:T(8,128)(2,1)S(1)}) custom-call(bf16[64,16,512]{2,1,0:T(8,128)(2,1)S(1)} %all_to_all.20.recv_ref, bf16[512,512]{1,0:T(8,128)(2,1)S(1)} %get-tuple-element.16.stack_ref, ...), custom_call_target="tpu_custom_call" | custom-call | flops 536870912 | bytes 5242880 | tf_op jit(solution)/shard_map/terms/pallas_call | solution.py:196
  68.9 2.1 %collective-permute-start = (bf16[16,128,128]{2,1,0:T(8,128)(2,1)S(1)}, bf16[16,128,128]{2,1,0:T(8,128)(2,1)S(1)}, u32[]{:S(2)}, u32[]{:S(2)}) collective-permute-start(bf16[16,128,128]{2,1,0:T(8,128)(2,1)S(1)} %get-tuple-element.23), channel_id=1, source_target_pairs={{0,8},{8,0},{1,9},{9,1},{2,10},{10,2},{3,11},{11,3},{4,12},{12,4},... | collective-permute-start | bytes 1572872 | tf_op jit(solution)/shard_map/ppermute | solution.py:213
  71.0 1.7 %collective-permute-done.recv_ref = bf16[16,128,128]{2,1,0:T(8,128)(2,1)S(1)} collective-permute-done((bf16[16,128,128]{2,1,0:T(8,128)(2,1)S(1)}, bf16[16,128,128]{2,1,0:T(8,128)(2,1)S(1)}, u32[]{:S(2)}, u32[]{:S(2)}) %collective-permute-start) | collective-permute-done | bytes 524320 | tf_op jit(solution)/shard_map/ppermute | solution.py:213
  72.7 0.1 pair_sum.1
  72.8 0.0 copy-start.1
  72.8 0.0 copy-start.2
  72.8 20.8 %all_to_all.21.recv_ref = bf16[16,128,128]{2,1,0:T(8,128)(2,1)S(1)} all-to-all(bf16[16,128,128]{2,1,0:T(8,128)(2,1)S(1)} %pair_sum.1), channel_id=1, replica_groups=mesh['zl'=8,'x'=4,'core'=2,'zh'=2,'y'=4] {'x','y'}, dimensions={0} | all-to-all | bytes 1048576 | tf_op jit(solution)/shard_map/all_to_all | solution.py:167
  93.6 0.0 copy-start
  93.6 0.1 plane_sum.1
  93.7 21.2 %all_to_all.22.recv_ref = bf16[16,16,128]{2,1,0:T(8,128)(2,1)S(1)} all-to-all(bf16[16,16,128]{2,1,0:T(8,128)(2,1)S(1)} %plane_sum.1), channel_id=1, replica_groups=mesh['zl'=8,'x'=4,'core'=2,'zh'=2,'y'=4] {'zl','zh'}, dimensions={0} | all-to-all | bytes 131072 | tf_op jit(solution)/shard_map/all_to_all | solution.py:167
  114.9 0.6 line_sum.1
  115.5 3.3 %all-to-all-start.3 = ((f32[4,16,128]{2,1,0:T(8,128)}), f32[4,16,128]{2,1,0:T(8,128)S(1)}, u32[]{:S(2)}, u32[]{:S(2)}) async-start(f32[4,16,128]{2,1,0:T(8,128)} %line_sum.1), calls=%async_computation.3 | async-start | bytes 65536 | tf_op jit(solution)/shard_map/all_to_all | solution.py:167
  118.8 0.0 copy-done.1
  118.8 0.0 copy-done.2
  118.8 0.0 copy-done
  118.8 1.6 %grads.1 = (bf16[64,4096]{1,0:T(8,128)(2,1)}, bf16[64,4096]{1,0:T(8,128)(2,1)}) custom-call(bf16[512,512]{1,0:T(8,128)(2,1)S(1)} %get-tuple-element.18.za_ref, bf16[512,512]{1,0:T(8,128)(2,1)S(1)} %get-tuple-element.19.zb_ref, bf16[64,4096]{1,0:T(8,128)(2,1)S(1)} %copy-done, bf16[512,512]{1,0:T(8,128)(2,1)S(1)} %copy-done.1, bf16[512,512]{1,0:T(8,128)(2,1)S(1)} %copy-done.2), custom_call_target="tpu_custom_call" | custom-call | flops 536870912 | bytes 4194304 | tf_op jit(solution)/shard_map/grads/pallas_call | solution.py:216
  120.4 3.8 %all-to-all-done.3.recv_ref = f32[4,16,128]{2,1,0:T(8,128)S(1)} async-done(((f32[4,16,128]{2,1,0:T(8,128)}), f32[4,16,128]{2,1,0:T(8,128)S(1)}, u32[]{:S(2)}, u32[]{:S(2)}) %all-to-all-start.3) | async-done | bytes 32800 | tf_op jit(solution)/shard_map/all_to_all | solution.py:167
  124.2 0.6 last.1
Async XLA Ops:
  68.9 3.8 %collective-permute-start = (bf16[16,128,128]{2,1,0:T(8,128)(2,1)S(1)}, bf16[16,128,128]{2,1,0:T(8,128)(2,1)S(1)}, u32[]{:S(2)}, u32[]{:S(2)}) collective-permute-start(bf16[16,128,128]{2,1,0:T(8,128)(2,1)S(1)} %get-tuple-element.23), channel_id=1, source_target_pairs={{0,8},{8,0},{1,9},{9,1},{2,10},{10,2},{3,11},{11,3},{4,12},{12,4},... | collective-permute-start | bytes 1572872 | tf_op jit(solution)/shard_map/ppermute | solution.py:213
  72.8 46.0 %copy-start.1 = (bf16[512,512]{1,0:T(8,128)(2,1)S(1)}, bf16[512,512]{1,0:T(8,128)(2,1)}, u32[]{:S(2)}) copy-start(bf16[512,512]{1,0:T(8,128)(2,1)} %first_ref.1) | copy-start | bytes 1572868
  72.8 46.0 %copy-start.2 = (bf16[512,512]{1,0:T(8,128)(2,1)S(1)}, bf16[512,512]{1,0:T(8,128)(2,1)}, u32[]{:S(2)}) copy-start(bf16[512,512]{1,0:T(8,128)(2,1)} %second_ref.1) | copy-start | bytes 1572868
  93.6 25.2 %copy-start = (bf16[64,4096]{1,0:T(8,128)(2,1)S(1)}, bf16[64,4096]{1,0:T(8,128)(2,1)}, u32[]{:S(2)}) copy-start(bf16[64,4096]{1,0:T(8,128)(2,1)} %g_ref.1) | copy-start | bytes 1572868
  115.5 8.7 %all-to-all-start.3 = ((f32[4,16,128]{2,1,0:T(8,128)}), f32[4,16,128]{2,1,0:T(8,128)S(1)}, u32[]{:S(2)}, u32[]{:S(2)}) async-start(f32[4,16,128]{2,1,0:T(8,128)} %line_sum.1), calls=%async_computation.3 | async-start | bytes 65536 | tf_op jit(solution)/shard_map/all_to_all | solution.py:167

commit v3 on v2

--- a/solution.py
+++ b/solution.py
@@ -8,7 +8,7 @@
 
 BF = jnp.bfloat16
 F32 = jnp.float32
-SEQ = ("zl", "x", "core")
+SEQ = ("zb", "za", "x", "core")
 CHAN = ("zh", "y")
 LANES = 128
 
@@ -37,7 +37,7 @@
 
 
 def send_kernel(
-    x_hbm, g_hbm, q_hbm, first_hbm, second_hbm, out_ref, stack_ref, mixer_ref, x_ref, g_ref, q_ref, first_ref, second_ref, sems
+    x_hbm, g_hbm, q_hbm, first_hbm, second_hbm, out_ref, stack_ref, mixer_ref, g_ref, first_ref, second_ref, x_ref, q_ref, sems
 ):
     pairs = ((x_hbm, x_ref), (first_hbm, first_ref), (g_hbm, g_ref), (q_hbm, q_ref), (second_hbm, second_ref))
     copies = [pltpu.make_async_copy(src, dst, sems.at[n]) for n, (src, dst) in enumerate(pairs)]
@@ -78,7 +78,7 @@
     return jnp.concatenate([result[pair].astype(BF) for pair in range(own // 2)], axis=1)
 
 
-def terms_kernel(recv_ref, stack_ref, mixer_ref, keep_ref, send_ref, za_ref, zb_ref, scratch, result, halves):
+def terms_kernel(recv_ref, stack_ref, mixer_ref, keep_ref, send_ref, za_ref, zb_ref, scratch, result, terms):
     count, both, width = recv_ref.shape
     own = both // 2
     received = recv_ref[...].astype(F32)
@@ -86,26 +86,29 @@
     za_ref[...] = za
     zb = regroup(received[:, own:], scratch, result)
     zb_ref[...] = zb
-    first = dot(zb, stack_ref[...], ((1,), (0,)))
-    second = dot(mixer_ref[...], za, ((0,), (1,)))
+    terms[0] = dot(zb, stack_ref[...], ((1,), (0,)))
+    terms[1] = dot(mixer_ref[...], za, ((0,), (1,)))
     targets, lines, lanes = keep_ref.shape
-    pieces = first.shape[1] // lanes
-    across = targets // pieces
-    for core in range(2):
-        for x in range(across):
-            for piece in range(pieces):
-                starts = [((z * across + x) * 2 + core) * 8 for z in range(lines // 16)]
-                halves[core, x * pieces + piece] = jnp.concatenate(
-                    [
-                        term[start:start + 8, piece * lanes:(piece + 1) * lanes]
-                        for term in (first, second)
-                        for start in starts
-                    ],
-                    axis=0,
-                )
+    pieces = terms.shape[2] // lanes
+    blocks = lines // 16
+    across = targets // (2 * pieces)
     core = lax.axis_index("core")
-    keep_ref[...] = halves[core]
-    send_ref[...] = halves[1 - core].astype(BF)
+    for x in range(across):
+        for piece in range(pieces):
+            for za in range(2):
+                for ref, line in ((keep_ref, core), (send_ref, 1 - core)):
+                    ref[(x * pieces + piece) * 2 + za] = jnp.concatenate(
+                        [
+                            terms[
+                                factor,
+                                pl.ds(pl.multiple_of((2 * ((2 * zb + za) * across + x) + line) * 8, 8), 8),
+                                piece * lanes:(piece + 1) * lanes,
+                            ]
+                            for factor in range(2)
+                            for zb in range(blocks)
+                        ],
+                        axis=0,
+                    ).astype(ref.dtype)
 
 
 def pair_kernel(keep_ref, recv_ref, out_ref):
@@ -125,30 +128,27 @@
         input_ref[:, i * cols:(i + 1) * cols] = grad[i * chan:(i + 1) * chan].astype(BF)
 
 
-def plane_kernel(recv_ref, out_ref):
+def block_kernel(recv_ref, out_ref):
     total = recv_ref[0].astype(F32)
     for source in range(1, recv_ref.shape[0]):
         total += recv_ref[source].astype(F32)
-    lines = out_ref.shape[0] // 2
-    for z in range(lines):
-        piece = jnp.concatenate([total[z * 8:z * 8 + 8], total[(lines + z) * 8:(lines + z) * 8 + 8]], axis=0)
-        for copy in range(2):
-            out_ref[2 * z + copy] = piece.astype(out_ref.dtype)
-
-
-def line_kernel(recv_ref, out_ref):
-    total = recv_ref[0].astype(F32)
-    for source in range(1, recv_ref.shape[0]):
-        total += recv_ref[source].astype(F32)
-    for copy in range(out_ref.shape[0]):
-        out_ref[copy] = total
+    blocks = recv_ref.shape[1] // 16
+    copies = out_ref.shape[0] // blocks
+    for zb in range(blocks):
+        piece = jnp.concatenate([total[zb * 8:zb * 8 + 8], total[(blocks + zb) * 8:(blocks + zb) * 8 + 8]], axis=0)
+        for copy in range(copies):
+            out_ref[zb * copies + copy] = piece.astype(BF)
 
 
 def last_kernel(recv_ref, first_ref, second_ref):
-    for piece in range(recv_ref.shape[0]):
+    pieces = first_ref.shape[1] // LANES
+    for piece in range(pieces):
+        total = recv_ref[piece].astype(F32)
+        for source in range(1, recv_ref.shape[0] // pieces):
+            total += recv_ref[source * pieces + piece].astype(F32)
         span = slice(piece * LANES, (piece + 1) * LANES)
-        first_ref[:, span] = recv_ref[piece, 0:8]
-        second_ref[:, span] = recv_ref[piece, 8:16]
+        first_ref[:, span] = total[0:8]
+        second_ref[:, span] = total[8:16]
 
 
 def call(kernel, out_shape, name, scratch=(), flops=0, data=0, vmem=40 << 20, **specs):
@@ -174,19 +174,27 @@
     rows = second_factor.shape[0]
     own = extent // cols
     width = own * chan
-    lines, copies = lax.axis_size("zl"), lax.axis_size("zh")
-    pieces = lax.axis_size("y")
-    planes = count // lines
+    blocks = lax.axis_size("zb")
+    near = lax.axis_size(("x", "y", "za"))
+    share = (near, 2 * blocks * 8, LANES)
+    copies = lax.axis_size(("zh", "y"))
     shape = jax.ShapeDtypeStruct
     given = tuple(
         pltpu.with_memory_space_constraint(value, pltpu.HBM)
         for value in (inputs, out_grad, gate_acts, first_factor, second_factor)
     )
-    sent, stack, mixer = call(
+    sent, stack, mixer, cotangent, first_near, second_near = call(
         send_kernel,
-        (shape((count, 2 * own, width), BF), shape((width, cols), BF), shape((width, rows), BF)),
+        (
+            shape((count, 2 * own, width), BF),
+            shape((width, cols), BF),
+            shape((width, rows), BF),
+            shape(out_grad.shape, BF),
+            shape(first_factor.shape, BF),
+            shape(second_factor.shape, BF),
+        ),
         "send",
-        scratch=[pltpu.VMEM(value.shape, BF) for value in given] + [pltpu.SemaphoreType.DMA((len(given),))],
+        scratch=[pltpu.VMEM(inputs.shape, BF), pltpu.VMEM(gate_acts.shape, BF), pltpu.SemaphoreType.DMA((len(given),))],
         flops=2 * 2 * rows * cols * width,
         data=5 << 20,
         in_specs=[pl.BlockSpec(memory_space=pltpu.HBM)] * len(given),
@@ -196,8 +204,8 @@
     keep, send, za, zb = call(
         terms_kernel,
         (
-            shape((planes // 2 * pieces, 2 * lines * 8, LANES), F32),
-            shape((planes // 2 * pieces, 2 * lines * 8, LANES), BF),
+            shape(share, F32),
+            shape(share, BF),
             shape((rows, width), BF),
             shape((cols, width), BF),
         ),
@@ -205,33 +213,32 @@
         scratch=[
             pltpu.VMEM((groups, rows, LANES), F32),
             pltpu.VMEM((own // 2, rows, LANES), F32),
-            pltpu.VMEM((2, planes // 2 * pieces, 2 * lines * 8, LANES), F32),
+            pltpu.VMEM((2, rows, cols), F32),
         ],
         flops=2 * 2 * rows * cols * width,
         data=5 << 20,
     )(received, stack, mixer)
     other = lax.ppermute(send, "core", [(0, 1), (1, 0)])
     paired = call(pair_kernel, shape(send.shape, BF), "pair_sum", data=2 << 20)(keep, other)
-    plane = exchange(paired, ("x", "y"))
     input_grad, gate_grad = call(
         grads_kernel,
         (shape((chan, extent), BF), shape((chan, extent), BF)),
         "grads",
         flops=2 * 2 * rows * cols * width,
         data=4 << 20,
-    )(za, zb, out_grad, first_factor, second_factor)
-    partial = call(plane_kernel, shape((lines * copies, 16, LANES), BF), "plane_sum", data=1 << 20)(plane)
-    line = exchange(partial, ("zl", "zh"))
-    summed = call(line_kernel, shape((pieces, 16, LANES), F32), "line_sum", data=1 << 17)(line)
-    gathered = exchange(summed, "y")
+    )(za, zb, cotangent, first_near, second_near)
+    paired, input_grad, gate_grad = lax.optimization_barrier((paired, input_grad, gate_grad))
+    block = exchange(paired, ("x", "y", "za"))
+    partial = call(block_kernel, shape((blocks * copies, 16, LANES), BF), "block_sum", data=1 << 20)(block)
+    spread = exchange(partial, ("zb", "zh", "y"))
     first_grad, second_grad = call(
-        last_kernel, (shape((8, cols), F32), shape((8, rows), F32)), "last", data=1 << 16
-    )(gathered)
+        last_kernel, (shape((8, cols), F32), shape((8, rows), F32)), "last", data=1 << 17
+    )(spread)
     return (input_grad, gate_grad, first_grad, second_grad)
 
 
 def solution(mesh):
-    fine = Mesh(mesh.devices.reshape(8, 4, 2, 2, 4), SEQ + CHAN)
+    fine = Mesh(mesh.devices.reshape(4, 2, 4, 2, 2, 4), SEQ + CHAN)
     return jax.shard_map(
         local,
         mesh=fine,

time: 125 us -> 120 us (0.960)
  the two profiles are of different devices: /device:TPU:32 before, /device:TPU:1 now
where the time goes in v3:
time: 120 us; the launch traced here: 119 us
  blocking collectives  110 us (92%)
  Pallas kernels  6.54 us (5%)
  starting transfers between devices  2.15 us (2%)
    all_to_all x3, blocking collectives, exchange(): return lax.all_to_all(value, axes, split_axis=0, concat_axis=0, tiled=True)  110 us
  transfers between devices with their start and end apart: 1, of which 1 were waited for; matrix products, arithmetic and copies ran while one was open for 0% of the time, Pallas kernels for 1%

profile of v3, /device:TPU:1, one launch (start us, length us, event | category | flops | bytes accessed | tf_op | source)
XLA Modules:
  0.0 119.3 jit_solution(5070406883634000075)
XLA Ops:
  0.6 2.4 %send.1 = (bf16[64,16,512]{2,1,0:T(8,128)(2,1)S(1)}, bf16[512,512]{1,0:T(8,128)(2,1)S(1)}, bf16[512,512]{1,0:T(8,128)(2,1)S(1)}, bf16[64,4096]{1,0:T(8,128)(2,1)...) custom-call(bf16[64,4096]{1,0:T(8,128)(2,1)} %x_hbm.1, bf16[64,4096]{1,0:T(8,128)(2,1)} %g_hbm.1, ...), custom_call_target="tpu_custom_call" | custom-call | flops 536870912 | bytes 5242880 | tf_op jit(solution)/shard_map/send/pallas_call | solution.py:186
  3.0 68.3 %all_to_all.15.recv_ref = bf16[64,16,512]{2,1,0:T(8,128)(2,1)S(1)} all-to-all(bf16[64,16,512]{2,1,0:T(8,128)(2,1)S(1)} %get-tuple-element.21), channel_id=1, replica_groups=mesh['zb'=4,'za'=2,'x'=4,'core'=2,'zh'=2,'y'=4] {'zb','za','x','core'}, dimensions={0} | all-to-all | bytes 2097152 | tf_op jit(solution)/shard_map/all_to_all | solution.py:167
  71.3 1.8 %terms.1 = (f32[32,64,128]{2,1,0:T(8,128)S(1)}, bf16[32,64,128]{2,1,0:T(8,128)(2,1)S(1)}, bf16[512,512]{1,0:T(8,128)(2,1)S(1)}, bf16[512,512]{1,0:T(8,128)(2,1)S(1)}) custom-call(bf16[64,16,512]{2,1,0:T(8,128)(2,1)S(1)} %all_to_all.15.recv_ref, bf16[512,512]{1,0:T(8,128)(2,1)S(1)} %get-tuple-element.22.stack_ref, ...), custom_call_target="tpu_custom_call" | custom-call | flops 536870912 | bytes 5242880 | tf_op jit(solution)/shard_map/terms/pallas_call | solution.py:204
  73.2 2.1 %collective-permute-start = (bf16[32,64,128]{2,1,0:T(8,128)(2,1)S(1)}, bf16[32,64,128]{2,1,0:T(8,128)(2,1)S(1)}, u32[]{:S(2)}, u32[]{:S(2)}) collective-permute-start(bf16[32,64,128]{2,1,0:T(8,128)(2,1)S(1)} %get-tuple-element.25), channel_id=1, source_target_pairs={{0,8},{8,0},{1,9},{9,1},{2,10},{10,2},{3,11},{11,3},{4,12},{12,4},... | collective-permute-start | bytes 1572872 | tf_op jit(solution)/shard_map/ppermute | solution.py:221
  75.3 1.5 %grads.1 = (bf16[64,4096]{1,0:T(8,128)(2,1)}, bf16[64,4096]{1,0:T(8,128)(2,1)}) custom-call(bf16[512,512]{1,0:T(8,128)(2,1)S(1)} %get-tuple-element.26.za_ref, bf16[512,512]{1,0:T(8,128)(2,1)S(1)} %get-tuple-element.27.zb_ref, bf16[64,4096]{1,0:T(8,128)(2,1)S(1)} %get-tuple-element.28.g_ref, bf16[512,512]{1,0:T(8,128)(2,1)S(1)} %get-tuple-element.29.first_ref, ...), custom_call_target="tpu_custom_call" | custom-call | flops 536870912 | bytes 4194304 | tf_op jit(solution)/shard_map/grads/pallas_call | solution.py:223
  76.9 0.1 collective-permute-done.recv_ref
  77.0 0.1 pair_sum.1
  77.1 18.4 %all_to_all.16.recv_ref = bf16[32,64,128]{2,1,0:T(8,128)(2,1)S(1)} all-to-all(bf16[32,64,128]{2,1,0:T(8,128)(2,1)S(1)} %pair_sum.1), channel_id=1, replica_groups=mesh['zb'=4,'za'=2,'x'=4,'core'=2,'zh'=2,'y'=4] {'x','y','za'}, dimensions={0} | all-to-all | bytes 1048576 | tf_op jit(solution)/shard_map/all_to_all | solution.py:167
  95.4 0.1 block_sum.1
  95.5 23.2 %all_to_all.17.recv_ref = bf16[32,16,128]{2,1,0:T(8,128)(2,1)S(1)} all-to-all(bf16[32,16,128]{2,1,0:T(8,128)(2,1)S(1)} %block_sum.1), channel_id=1, replica_groups=mesh['zb'=4,'za'=2,'x'=4,'core'=2,'zh'=2,'y'=4] {'zb','zh','y'}, dimensions={0} | all-to-all | bytes 262144 | tf_op jit(solution)/shard_map/all_to_all | solution.py:167
  118.7 0.6 last.1
Async XLA Ops:
  73.2 3.8 %collective-permute-start = (bf16[32,64,128]{2,1,0:T(8,128)(2,1)S(1)}, bf16[32,64,128]{2,1,0:T(8,128)(2,1)S(1)}, u32[]{:S(2)}, u32[]{:S(2)}) collective-permute-start(bf16[32,64,128]{2,1,0:T(8,128)(2,1)S(1)} %get-tuple-element.25), channel_id=1, source_target_pairs={{0,8},{8,0},{1,9},{9,1},{2,10},{10,2},{3,11},{11,3},{4,12},{12,4},... | collective-permute-start | bytes 1572872 | tf_op jit(solution)/shard_map/ppermute | solution.py:221

commit v4 on v3

--- a/solution.py
+++ b/solution.py
@@ -39,7 +39,7 @@
 def send_kernel(
     x_hbm, g_hbm, q_hbm, first_hbm, second_hbm, out_ref, stack_ref, mixer_ref, g_ref, first_ref, second_ref, x_ref, q_ref, sems
 ):
-    pairs = ((x_hbm, x_ref), (first_hbm, first_ref), (g_hbm, g_ref), (q_hbm, q_ref), (second_hbm, second_ref))
+    pairs = ((first_hbm, first_ref), (x_hbm, x_ref), (second_hbm, second_ref), (g_hbm, g_ref), (q_hbm, q_ref))
     copies = [pltpu.make_async_copy(src, dst, sems.at[n]) for n, (src, dst) in enumerate(pairs)]
     for copy in copies:
         copy.start()
@@ -47,15 +47,14 @@
     rows = second_ref.shape[0]
     count, both, width = out_ref.shape
     copies[0].wait()
+    copies[1].wait()
     stack = stacked(x_ref, cols)
     stack_ref[...] = stack
-    copies[1].wait()
     inner = dot(first_ref[...], stack, ((1,), (1,)))
-    copies[2].wait()
-    copies[3].wait()
+    for copy in copies[2:]:
+        copy.wait()
     mixer = product_stacked(g_ref, q_ref, rows)
     mixer_ref[...] = mixer
-    copies[4].wait()
     back = dot(second_ref[...], mixer, ((0,), (1,)))
     out_ref[...] = jnp.concatenate(
         [inner.reshape(count, both // 2, width), back.reshape(count, both // 2, width)], axis=1
@@ -97,7 +96,7 @@
         for piece in range(pieces):
             for za in range(2):
                 for ref, line in ((keep_ref, core), (send_ref, 1 - core)):
-                    ref[(x * pieces + piece) * 2 + za] = jnp.concatenate(
+                    ref[(za * pieces + piece) * across + x] = jnp.concatenate(
                         [
                             terms[
                                 factor,
@@ -228,7 +227,7 @@
         data=4 << 20,
     )(za, zb, cotangent, first_near, second_near)
     paired, input_grad, gate_grad = lax.optimization_barrier((paired, input_grad, gate_grad))
-    block = exchange(paired, ("x", "y", "za"))
+    block = exchange(paired, ("za", "y", "x"))
     partial = call(block_kernel, shape((blocks * copies, 16, LANES), BF), "block_sum", data=1 << 20)(block)
     spread = exchange(partial, ("zb", "zh", "y"))
     first_grad, second_grad = call(

time: 120 us -> 121 us (level)
  no operation moved by 1% of the time
where the time goes in v4:
time: 121 us; the launch traced here: 120 us
  blocking collectives  111 us (92%)
  Pallas kernels  6.46 us (5%)
  starting transfers between devices  2.15 us (2%)
    all_to_all x3, blocking collectives, exchange(): return lax.all_to_all(value, axes, split_axis=0, concat_axis=0, tiled=True)  111 us
  transfers between devices with their start and end apart: 1, of which 1 were waited for; matrix products, arithmetic and copies ran while one was open for 0% of the time, Pallas kernels for 1%

profile of v4, /device:TPU:1, one launch (start us, length us, event | category | flops | bytes accessed | tf_op | source)
XLA Modules:
  0.0 120.3 jit_solution(14114575204053015162)
XLA Ops:
  0.6 2.3 %send.1 = (bf16[64,16,512]{2,1,0:T(8,128)(2,1)S(1)}, bf16[512,512]{1,0:T(8,128)(2,1)S(1)}, bf16[512,512]{1,0:T(8,128)(2,1)S(1)}, bf16[64,4096]{1,0:T(8,128)(2,1)...) custom-call(bf16[64,4096]{1,0:T(8,128)(2,1)} %x_hbm.1, bf16[64,4096]{1,0:T(8,128)(2,1)} %g_hbm.1, ...), custom_call_target="tpu_custom_call" | custom-call | flops 536870912 | bytes 5242880 | tf_op jit(solution)/shard_map/send/pallas_call | solution.py:185
  2.9 68.3 %all_to_all.15.recv_ref = bf16[64,16,512]{2,1,0:T(8,128)(2,1)S(1)} all-to-all(bf16[64,16,512]{2,1,0:T(8,128)(2,1)S(1)} %get-tuple-element.21), channel_id=1, replica_groups=mesh['zb'=4,'za'=2,'x'=4,'core'=2,'zh'=2,'y'=4] {'zb','za','x','core'}, dimensions={0} | all-to-all | bytes 2097152 | tf_op jit(solution)/shard_map/all_to_all | solution.py:166
  71.2 1.8 %terms.1 = (f32[32,64,128]{2,1,0:T(8,128)S(1)}, bf16[32,64,128]{2,1,0:T(8,128)(2,1)S(1)}, bf16[512,512]{1,0:T(8,128)(2,1)S(1)}, bf16[512,512]{1,0:T(8,128)(2,1)S(1)}) custom-call(bf16[64,16,512]{2,1,0:T(8,128)(2,1)S(1)} %all_to_all.15.recv_ref, bf16[512,512]{1,0:T(8,128)(2,1)S(1)} %get-tuple-element.22.stack_ref, ...), custom_call_target="tpu_custom_call" | custom-call | flops 536870912 | bytes 5242880 | tf_op jit(solution)/shard_map/terms/pallas_call | solution.py:203
  73.1 2.1 %collective-permute-start = (bf16[32,64,128]{2,1,0:T(8,128)(2,1)S(1)}, bf16[32,64,128]{2,1,0:T(8,128)(2,1)S(1)}, u32[]{:S(2)}, u32[]{:S(2)}) collective-permute-start(bf16[32,64,128]{2,1,0:T(8,128)(2,1)S(1)} %get-tuple-element.25), channel_id=1, source_target_pairs={{0,8},{8,0},{1,9},{9,1},{2,10},{10,2},{3,11},{11,3},{4,12},{12,4},... | collective-permute-start | bytes 1572872 | tf_op jit(solution)/shard_map/ppermute | solution.py:220
  75.2 1.6 %grads.1 = (bf16[64,4096]{1,0:T(8,128)(2,1)}, bf16[64,4096]{1,0:T(8,128)(2,1)}) custom-call(bf16[512,512]{1,0:T(8,128)(2,1)S(1)} %get-tuple-element.26.za_ref, bf16[512,512]{1,0:T(8,128)(2,1)S(1)} %get-tuple-element.27.zb_ref, bf16[64,4096]{1,0:T(8,128)(2,1)S(1)} %get-tuple-element.28.g_ref, bf16[512,512]{1,0:T(8,128)(2,1)S(1)} %get-tuple-element.29.first_ref, ...), custom_call_target="tpu_custom_call" | custom-call | flops 536870912 | bytes 4194304 | tf_op jit(solution)/shard_map/grads/pallas_call | solution.py:222
  76.8 0.1 collective-permute-done.recv_ref
  76.9 0.1 pair_sum.1
  77.0 17.3 %all_to_all.16.recv_ref = bf16[32,64,128]{2,1,0:T(8,128)(2,1)S(1)} all-to-all(bf16[32,64,128]{2,1,0:T(8,128)(2,1)S(1)} %pair_sum.1), channel_id=1, replica_groups=mesh['zb'=4,'za'=2,'x'=4,'core'=2,'zh'=2,'y'=4] {'za','y','x'}, dimensions={0} | all-to-all | bytes 1048576 | tf_op jit(solution)/shard_map/all_to_all | solution.py:166
  94.3 0.1 block_sum.1
  94.3 25.3 %all_to_all.17.recv_ref = bf16[32,16,128]{2,1,0:T(8,128)(2,1)S(1)} all-to-all(bf16[32,16,128]{2,1,0:T(8,128)(2,1)S(1)} %block_sum.1), channel_id=1, replica_groups=mesh['zb'=4,'za'=2,'x'=4,'core'=2,'zh'=2,'y'=4] {'zb','zh','y'}, dimensions={0} | all-to-all | bytes 262144 | tf_op jit(solution)/shard_map/all_to_all | solution.py:166
  119.6 0.6 last.1
Async XLA Ops:
  73.1 3.8 %collective-permute-start = (bf16[32,64,128]{2,1,0:T(8,128)(2,1)S(1)}, bf16[32,64,128]{2,1,0:T(8,128)(2,1)S(1)}, u32[]{:S(2)}, u32[]{:S(2)}) collective-permute-start(bf16[32,64,128]{2,1,0:T(8,128)(2,1)S(1)} %get-tuple-element.25), channel_id=1, source_target_pairs={{0,8},{8,0},{1,9},{9,1},{2,10},{10,2},{3,11},{11,3},{4,12},{12,4},... | collective-permute-start | bytes 1572872 | tf_op jit(solution)/shard_map/ppermute | solution.py:220

commit v5 on v4

--- a/solution.py
+++ b/solution.py
@@ -83,10 +83,10 @@
     received = recv_ref[...].astype(F32)
     za = regroup(received[:, :own], scratch, result)
     za_ref[...] = za
+    terms[1] = dot(mixer_ref[...], za, ((0,), (1,)))
     zb = regroup(received[:, own:], scratch, result)
     zb_ref[...] = zb
     terms[0] = dot(zb, stack_ref[...], ((1,), (0,)))
-    terms[1] = dot(mixer_ref[...], za, ((0,), (1,)))
     targets, lines, lanes = keep_ref.shape
     pieces = terms.shape[2] // lanes
     blocks = lines // 16

time: 121 us -> 120 us (level)
  no operation moved by 1% of the time
where the time goes in v5:
time: 120 us
  blocking collectives  111 us (92%)
  Pallas kernels  6.22 us (5%)
  starting transfers between devices  2.17 us (2%)
    all_to_all x3, blocking collectives, exchange(): return lax.all_to_all(value, axes, split_axis=0, concat_axis=0, tiled=True)  111 us
  transfers between devices with their start and end apart: 1, of which 1 were waited for; matrix products, arithmetic and copies ran while one was open for 0% of the time, Pallas kernels for 1%

profile of v5, /device:TPU:1, one launch (start us, length us, event | category | flops | bytes accessed | tf_op | source)
XLA Modules:
  0.0 120.0 jit_solution(1101022517611060903)
XLA Ops:
  0.6 2.3 %send.1 = (bf16[64,16,512]{2,1,0:T(8,128)(2,1)S(1)}, bf16[512,512]{1,0:T(8,128)(2,1)S(1)}, bf16[512,512]{1,0:T(8,128)(2,1)S(1)}, bf16[64,4096]{1,0:T(8,128)(2,1)...) custom-call(bf16[64,4096]{1,0:T(8,128)(2,1)} %x_hbm.1, bf16[64,4096]{1,0:T(8,128)(2,1)} %g_hbm.1, ...), custom_call_target="tpu_custom_call" | custom-call | flops 536870912 | bytes 5242880 | tf_op jit(solution)/shard_map/send/pallas_call | solution.py:185
  2.9 68.3 %all_to_all.15.recv_ref = bf16[64,16,512]{2,1,0:T(8,128)(2,1)S(1)} all-to-all(bf16[64,16,512]{2,1,0:T(8,128)(2,1)S(1)} %get-tuple-element.21), channel_id=1, replica_groups=mesh['zb'=4,'za'=2,'x'=4,'core'=2,'zh'=2,'y'=4] {'zb','za','x','core'}, dimensions={0} | all-to-all | bytes 2097152 | tf_op jit(solution)/shard_map/all_to_all | solution.py:166
  71.2 1.6 %terms.1 = (f32[32,64,128]{2,1,0:T(8,128)S(1)}, bf16[32,64,128]{2,1,0:T(8,128)(2,1)S(1)}, bf16[512,512]{1,0:T(8,128)(2,1)S(1)}, bf16[512,512]{1,0:T(8,128)(2,1)S(1)}) custom-call(bf16[64,16,512]{2,1,0:T(8,128)(2,1)S(1)} %all_to_all.15.recv_ref, bf16[512,512]{1,0:T(8,128)(2,1)S(1)} %get-tuple-element.22.stack_ref, ...), custom_call_target="tpu_custom_call" | custom-call | flops 536870912 | bytes 5242880 | tf_op jit(solution)/shard_map/terms/pallas_call | solution.py:203
  72.8 2.2 %collective-permute-start = (bf16[32,64,128]{2,1,0:T(8,128)(2,1)S(1)}, bf16[32,64,128]{2,1,0:T(8,128)(2,1)S(1)}, u32[]{:S(2)}, u32[]{:S(2)}) collective-permute-start(bf16[32,64,128]{2,1,0:T(8,128)(2,1)S(1)} %get-tuple-element.25), channel_id=1, source_target_pairs={{0,8},{8,0},{1,9},{9,1},{2,10},{10,2},{3,11},{11,3},{4,12},{12,4},... | collective-permute-start | bytes 1572872 | tf_op jit(solution)/shard_map/ppermute | solution.py:220
  75.0 1.5 %grads.1 = (bf16[64,4096]{1,0:T(8,128)(2,1)}, bf16[64,4096]{1,0:T(8,128)(2,1)}) custom-call(bf16[512,512]{1,0:T(8,128)(2,1)S(1)} %get-tuple-element.26.za_ref, bf16[512,512]{1,0:T(8,128)(2,1)S(1)} %get-tuple-element.27.zb_ref, bf16[64,4096]{1,0:T(8,128)(2,1)S(1)} %get-tuple-element.28.g_ref, bf16[512,512]{1,0:T(8,128)(2,1)S(1)} %get-tuple-element.29.first_ref, ...), custom_call_target="tpu_custom_call" | custom-call | flops 536870912 | bytes 4194304 | tf_op jit(solution)/shard_map/grads/pallas_call | solution.py:222
  76.6 0.1 collective-permute-done.recv_ref
  76.6 0.1 pair_sum.1
  76.7 17.3 %all_to_all.16.recv_ref = bf16[32,64,128]{2,1,0:T(8,128)(2,1)S(1)} all-to-all(bf16[32,64,128]{2,1,0:T(8,128)(2,1)S(1)} %pair_sum.1), channel_id=1, replica_groups=mesh['zb'=4,'za'=2,'x'=4,'core'=2,'zh'=2,'y'=4] {'za','y','x'}, dimensions={0} | all-to-all | bytes 1048576 | tf_op jit(solution)/shard_map/all_to_all | solution.py:166
  94.0 0.1 block_sum.1
  94.1 25.3 %all_to_all.17.recv_ref = bf16[32,16,128]{2,1,0:T(8,128)(2,1)S(1)} all-to-all(bf16[32,16,128]{2,1,0:T(8,128)(2,1)S(1)} %block_sum.1), channel_id=1, replica_groups=mesh['zb'=4,'za'=2,'x'=4,'core'=2,'zh'=2,'y'=4] {'zb','zh','y'}, dimensions={0} | all-to-all | bytes 262144 | tf_op jit(solution)/shard_map/all_to_all | solution.py:166
  119.4 0.6 last.1
Async XLA Ops:
  72.8 3.8 %collective-permute-start = (bf16[32,64,128]{2,1,0:T(8,128)(2,1)S(1)}, bf16[32,64,128]{2,1,0:T(8,128)(2,1)S(1)}, u32[]{:S(2)}, u32[]{:S(2)}) collective-permute-start(bf16[32,64,128]{2,1,0:T(8,128)(2,1)S(1)} %get-tuple-element.25), channel_id=1, source_target_pairs={{0,8},{8,0},{1,9},{9,1},{2,10},{10,2},{3,11},{11,3},{4,12},{12,4},... | collective-permute-start | bytes 1572872 | tf_op jit(solution)/shard_map/ppermute | solution.py:220
